TPU v7x, 512 devices: a whole 4x4x16 slice. The times are simulated.
512 devices in a mesh: slab: 128 (over y, z, core), sub: 4 (over x).
Axes of the slice: x: 4, y: 4, z: 16, core: 2. Of those that a mesh axis runs over, the one named last changes fastest.
Arguments:
- mode_shapes: bfloat16 [32, 6, 1024, 512], P(None, None, 'slab', 'sub')
- span_stiff: float32 [6, 1024, 512], P(None, 'slab', 'sub'), may hold values from -4 to 4
- chord_stiff: float32 [6, 1024, 512], P(None, 'slab', 'sub'), may hold values from -4 to 4
- span_geo: float32 [1024, 512], P('slab', 'sub'), may hold values from 0.2 to 2
- chord_geo: float32 [1024, 512], P('slab', 'sub'), may hold values from 0.2 to 2
- ground: float32 [6, 1024, 512], P(None, 'slab', 'sub'), may hold values from 0.2 to 2
- chord_len: int32 [1024], replicated, may hold values from 192 to 512, as said below
Outputs:
- adjoint: float32 [32, 6, 1024, 512], P(None, None, 'slab', 'sub')
- residual: float32 [32, 6, 1024, 512], P(None, None, 'slab', 'sub')
Inputs may be any that keep to these rules, and one draw needn't show every extreme that they name: chord_len[0] = 512.
All inputs are finite; a program needn't handle non-finite values.
Results may differ from a plain program's by a relative error of at most 0.0003.
Values sent between devices are 32-bit elements; how exact they have to be, the bound alone decides.
A program may use at most 64 MiB of HBM per device.

v0:
```python
import jax
import jax.numpy as jnp
from jax import lax
from jax.sharding import PartitionSpec as P

ITERS = 2


def from_behind(value, axis, steps):
    count = lax.axis_size(axis)
    initial, last = (max(0, -steps), min(count, count - steps))
    return lax.ppermute(value, axis, [(source, source + steps) for source in range(initial, last)])


def factor_blocks(blocks):
    count = len(blocks)
    factor = [[None] * count for i in range(count)]
    inverse = [None] * count
    for j in range(count):
        running = blocks[j][j]
        for k in range(j):
            running = running - factor[j][k] * factor[j][k]
        diag_root = jnp.sqrt(running)
        factor[j][j] = diag_root
        inverse[j] = 1.0 / diag_root
        for i in range(j + 1, count):
            running = blocks[i][j]
            for k in range(j):
                running = running - factor[i][k] * factor[j][k]
            factor[i][j] = running * inverse[j]
    return (factor, inverse)


def solve_blocks(factor, inverse, vector):
    count = len(inverse)
    forward = []
    for i in range(count):
        running = vector[:, i]
        for j in range(i):
            running = running - factor[i][j][None] * forward[j]
        forward.append(running * inverse[i][None])
    backward = [None] * count
    for i in reversed(range(count)):
        running = forward[i]
        for j in range(i + 1, count):
            running = running - factor[j][i][None] * backward[j]
        backward[i] = running * inverse[i][None]
    return jnp.stack(backward, axis=1)


def neighbours_ahead(field):
    next_station = from_behind(field[:, :, :1, :], "slab", -1)
    next_column = from_behind(field[:, :, :, :1], "sub", -1)
    span_next = jnp.concatenate([field[:, :, 1:, :], next_station], axis=2)
    chord_next = jnp.concatenate([field[:, :, :, 1:], next_column], axis=3)
    return (span_next, chord_next)


def forces_behind(span_forces, chord_forces):
    from_span = from_behind(span_forces[:, :, -1:, :], "slab", 1)
    from_chord = from_behind(chord_forces[:, :, :, -1:], "sub", 1)
    span_part = jnp.concatenate([from_span, span_forces[:, :, :-1, :]], axis=2)
    chord_part = jnp.concatenate([from_chord, chord_forces[:, :, :, :-1]], axis=3)
    return span_part + chord_part


def edge_forces(stiffness, jump, live_mask):
    strain = jnp.sum(stiffness[None] * jump, axis=1) * live_mask[None]
    return stiffness[None] * strain[:, None]


def operate_sent(field, span_stiff, chord_stiff, span_live, chord_live, ground):
    span_next, chord_next = neighbours_ahead(field)
    span_forces = edge_forces(span_stiff, span_next - field, span_live)
    chord_forces = edge_forces(chord_stiff, chord_next - field, chord_live)
    return (
        ground[None] * field - span_forces - chord_forces + forces_behind(span_forces, chord_forces)
    )


def inner_rz(first, second):
    return lax.psum(jnp.sum(first * second, axis=(1, 2, 3)), ("slab", "sub"))


def inner_pq(first, second):
    return lax.psum(jnp.sum(first * second, axis=(1, 2, 3)), ("slab", "sub"))


def body(mode_shapes, span_stiff, chord_stiff, span_geo, chord_geo, ground, chord_len):
    count = ground.shape[0]
    stations = ground.shape[1]
    columns = ground.shape[2]
    row_start = lax.axis_index("slab") * stations
    col_start = lax.axis_index("sub") * columns
    padded_len = jnp.concatenate(
        [jnp.zeros((1,), jnp.int32), chord_len, jnp.zeros((2,), jnp.int32)]
    )
    window = lax.dynamic_slice_in_dim(padded_len, row_start, stations + 2)
    col_global = (col_start + jnp.arange(columns, dtype=jnp.int32))[None, :]
    span_mask_wide = ((col_global < window[:-1, None]) & (col_global < window[1:, None])).astype(
        jnp.float32
    )
    col_wide = (col_start - 1 + jnp.arange(columns + 1, dtype=jnp.int32))[None, :]
    own_len = window[1 : stations + 1, None]
    chord_mask_wide = ((col_wide + 1 < own_len) & (col_wide >= 0)).astype(jnp.float32)
    span_live = span_mask_wide[1:]
    chord_live = chord_mask_wide[:, 1:]
    ghost_span = from_behind(span_stiff[:, stations - 1 :, :], "slab", 1)
    ghost_chord = from_behind(chord_stiff[:, :, columns - 1 :], "sub", 1)
    span_wide = jnp.concatenate([ghost_span, span_stiff], axis=1)
    chord_wide = jnp.concatenate([ghost_chord, chord_stiff], axis=2)
    blocks = []
    for i in range(count):
        block_row = []
        for j in range(count):
            span_pair = span_wide[i] * span_wide[j] * span_mask_wide
            chord_pair = chord_wide[i] * chord_wide[j] * chord_mask_wide
            entry = span_pair[1:] + span_pair[:-1] + chord_pair[:, 1:] + chord_pair[:, :-1]
            if i == j:
                entry = entry + ground[i]
            block_row.append(entry)
        blocks.append(block_row)
    factor, inverse = factor_blocks(blocks)
    mode_field = mode_shapes.astype(jnp.float32)
    span_next, chord_next = neighbours_ahead(mode_field)
    span_jump = span_next - mode_field
    chord_jump = chord_next - mode_field
    span_weight = jnp.sum(span_jump * span_jump, axis=1) * (span_geo * span_live)[None]
    chord_weight = jnp.sum(chord_jump * chord_jump, axis=1) * (chord_geo * chord_live)[None]
    span_load = span_stiff[None] * span_weight[:, None]
    chord_load = chord_stiff[None] * chord_weight[:, None]
    load = forces_behind(span_load, chord_load) - span_load - chord_load
    solution = jnp.zeros_like(load)
    residual = load
    precond = solve_blocks(factor, inverse, residual)
    direction = precond
    precond_norm = inner_rz(residual, precond)
    for step in range(ITERS):
        image = operate_sent(direction, span_stiff, chord_stiff, span_live, chord_live, ground)
        step_size = precond_norm / inner_pq(direction, image)
        solution = solution + step_size[:, None, None, None] * direction
        residual = residual - step_size[:, None, None, None] * image
        if step + 1 < ITERS:
            precond = solve_blocks(factor, inverse, residual)
            norm_next = inner_rz(residual, precond)
            direction = precond + (norm_next / precond_norm)[:, None, None, None] * direction
            precond_norm = norm_next
    return (solution, residual)


def solution(mesh):
    return jax.shard_map(
        body,
        mesh=mesh,
        in_specs=(
            P(None, None, "slab", "sub"),
            P(None, "slab", "sub"),
            P(None, "slab", "sub"),
            P("slab", "sub"),
            P("slab", "sub"),
            P(None, "slab", "sub"),
            P(),
        ),
        out_specs=(P(None, None, "slab", "sub"), P(None, None, "slab", "sub")),
        check_vma=False,
    )
```

profile of v0, /device:TPU:1, one launch (start us, length us, event | category | flops | bytes accessed | tf_op | source)
XLA Modules:
  0.0 413.0 jit_solution(10485907390977975643)
XLA Ops:
  1.4 4.9 %collective-permute-start.4 = (f32[6,1,128]{2,1,0:T(1,128)S(1)}, f32[6,1,128]{2,1,0:T(1,128)S(1)}, u32[]{:S(2)}, u32[]{:S(2)}) collective-permute-start(f32[6,1,128]{2,1,0:T(1,128)S(1)} %slice.527), channel_id=1, source_target_pairs={{0,4},{4,8},{8,12},{12,16},{16,20},{20,24},{24,28},{28,32},{32,36}... | collective-permute-start | bytes 9224 | tf_op jit(solution)/shard_map/ppermute | solution.py:12
  7.1 3.1 collective-permute-start.5
  13.0 3.3 collective-permute-start
  27.8 2.2 collective-permute-start.1
  30.8 4.0 collective-permute-start.3
  40.5 3.8 collective-permute-start.6
  46.7 1.6 fusion.9
  49.1 2.1 collective-permute-start.8
  52.5 2.1 copy.16
  54.6 4.4 %collective-permute-start.9 = (f32[32,6,8,1]{0,2,3,1:T(8,128)}, f32[32,6,8,1]{0,2,3,1:T(8,128)}, u32[]{:S(2)}, u32[]{:S(2)}) collective-permute-start(f32[32,6,8,1]{0,2,3,1:T(8,128)} %copy.16), channel_id=1, source_target_pairs={{0,1},{1,2},{2,3},{4,5},{5,6},{6,7},{8,9},{9,10},{10,11},{12,13},{... | collective-permute-start | bytes 18440 | tf_op jit(solution)/shard_map/ppermute | solution.py:12
  59.5 2.0 copy.17
  61.5 2.6 multiply_reduce_fusion.2
  64.1 112.9 %all-reduce = (f32[32]{0:T(128)S(1)}, f32[32]{0:T(128)S(1)}) all-reduce(f32[32]{0:T(128)S(1)} %get-tuple-element.7, f32[32]{0:T(128)S(1)} %get-tuple-element.6), channel_id=1, replica_groups=mesh['slab'=128,'sub'=4] {'slab','sub'}, use_global_device_ids=true, to_apply=%region_3.0 | all-reduce | flops 64 | bytes 512 | tf_op jit(solution)/shard_map/psum | solution.py:82
  180.0 98.7 %psum.30 = f32[32]{0:T(128)S(1)} all-reduce(f32[32]{0:T(128)S(1)} %multiply_reduce_fusion.1), channel_id=1, replica_groups=mesh['slab'=128,'sub'=4] {'slab','sub'}, use_global_device_ids=true, to_apply=%region_9.0 | all-reduce | flops 32 | bytes 256 | tf_op jit(solution)/shard_map/psum | solution.py:82
  278.9 2.6 collective-permute-start.10
  284.3 2.3 collective-permute-done.11
  287.9 1.8 fusion.14
  291.4 4.5 %collective-permute-start.12 = (f32[32,6,1,128]{3,0,2,1:T(8,128)}, f32[32,6,1,128]{3,0,2,1:T(8,128)}, u32[]{:S(2)}, u32[]{:S(2)}) collective-permute-start(f32[32,6,1,128]{3,0,2,1:T(8,128)} %slice.798), channel_id=1, source_target_pairs={{0,4},{4,8},{8,12},{12,16},{16,20},{20,24},{24,28},{28,32},{32,36}... | collective-permute-start | bytes 294920 | tf_op jit(solution)/shard_map/ppermute | solution.py:12
  297.1 1.5 copy.20
  298.6 2.9 collective-permute-start.13
  301.5 2.0 slice.799
  304.7 2.7 multiply_reduce_fusion
  307.5 100.6 %psum.31 = f32[32]{0:T(128)S(1)} all-reduce(f32[32]{0:T(128)S(1)} %get-tuple-element.14), channel_id=1, replica_groups=mesh['slab'=128,'sub'=4] {'slab','sub'}, use_global_device_ids=true, to_apply=%region_13.0 | all-reduce | flops 32 | bytes 256 | tf_op jit(solution)/shard_map/psum | solution.py:86
  408.8 1.5 multiply_subtract_fusion
  (167 shorter events, 41.6 us)
Async XLA Ops:
  1.4 20.2 %collective-permute-start.4 = (f32[6,1,128]{2,1,0:T(1,128)S(1)}, f32[6,1,128]{2,1,0:T(1,128)S(1)}, u32[]{:S(2)}, u32[]{:S(2)}) collective-permute-start(f32[6,1,128]{2,1,0:T(1,128)S(1)} %slice.527), channel_id=1, source_target_pairs={{0,4},{4,8},{8,12},{12,16},{16,20},{20,24},{24,28},{28,32},{32,36}... | collective-permute-start | bytes 9224 | tf_op jit(solution)/shard_map/ppermute | solution.py:12
  7.1 13.7 %collective-permute-start.5 = (f32[6,8,1]{2,1,0:T(8,128)S(1)}, f32[6,8,1]{2,1,0:T(8,128)S(1)}, u32[]{:S(2)}, u32[]{:S(2)}) collective-permute-start(f32[6,8,1]{2,1,0:T(8,128)S(1)} %slice.531), channel_id=1, source_target_pairs={{0,1},{1,2},{2,3},{4,5},{5,6},{6,7},{8,9},{9,10},{10,11},{12,13},{... | collective-permute-start | bytes 584 | tf_op jit(solution)/shard_map/ppermute | solution.py:12
  11.7 14.3 %collective-permute-start.2 = (f32[32,6,8,1]{0,2,3,1:T(8,128)S(1)}, f32[32,6,8,1]{0,2,3,1:T(8,128)S(1)}, u32[]{:S(2)}, u32[]{:S(2)}) collective-permute-start(f32[32,6,8,1]{0,2,3,1:T(8,128)S(1)} %copy.10), channel_id=1, source_target_pairs={{1,0},{2,1},{3,2},{5,4},{6,5},{7,6},{9,8},{10,9},{11,10},{13,12},{... | collective-permute-start | bytes 18440 | tf_op jit(solution)/shard_map/ppermute | solution.py:12
  13.0 13.4 %collective-permute-start = (f32[32,6,1,128]{3,0,2,1:T(8,128)S(1)}, f32[32,6,1,128]{3,0,2,1:T(8,128)S(1)}, u32[]{:S(2)}, u32[]{:S(2)}) collective-permute-start(f32[32,6,1,128]{3,0,2,1:T(8,128)S(1)} %slice.661), channel_id=1, source_target_pairs={{4,0},{8,4},{12,8},{16,12},{20,16},{24,20},{28,24},{32,28},{36,32}... | collective-permute-start | bytes 294920 | tf_op jit(solution)/shard_map/ppermute | solution.py:12
  21.6 3.2 copy-start.7
  27.8 7.1 %copy-start = (f32[32,6,8,128]{3,0,2,1:T(8,128)}, f32[32,6,8,128]{3,0,2,1:T(8,128)S(1)}, u32[]{:S(2)}) copy-start(f32[32,6,8,128]{3,0,2,1:T(8,128)S(1)} %broadcast_multiply_fusion.5) | copy-start | bytes 2359300
  27.8 2.3 copy-start.21
  27.8 8.3 %collective-permute-start.1 = (f32[32,6,1,128]{3,0,2,1:T(8,128)S(1)}, f32[32,6,1,128]{3,0,2,1:T(8,128)}, u32[]{:S(2)}, u32[]{:S(2)}) collective-permute-start(f32[32,6,1,128]{3,0,2,1:T(8,128)S(1)} %slice.663), channel_id=1, source_target_pairs={{0,4},{4,8},{8,12},{12,16},{16,20},{20,24},{24,28},{28,32},{32,36}... | collective-permute-start | bytes 294920 | tf_op jit(solution)/shard_map/ppermute | solution.py:12
  30.5 4.4 %copy-start.8 = (f32[8,129]{1,0:T(8,128)S(1)}, f32[8,129]{1,0:T(8,128)}, u32[]{:S(2)}) copy-start(f32[8,129]{1,0:T(8,128)} %copy-done.7) | copy-start | bytes 12388
  30.5 4.4 %copy-start.20 = (f32[8,128]{1,0:T(8,128)S(1)}, f32[8,128]{1,0:T(8,128)}, u32[]{:S(2)}) copy-start(f32[8,128]{1,0:T(8,128)} %copy-done.19) | copy-start | bytes 12292
  30.8 4.9 %collective-permute-start.3 = (f32[32,6,8,1]{0,2,3,1:T(8,128)S(1)}, f32[32,6,8,1]{0,2,3,1:T(8,128)S(1)}, u32[]{:S(2)}, u32[]{:S(2)}) collective-permute-start(f32[32,6,8,1]{0,2,3,1:T(8,128)S(1)} %copy.12), channel_id=1, source_target_pairs={{0,1},{1,2},{2,3},{4,5},{5,6},{6,7},{8,9},{9,10},{10,11},{12,13},{... | collective-permute-start | bytes 18440 | tf_op jit(solution)/shard_map/ppermute | solution.py:12
  38.8 5.5 %copy-start.24 = (pred[9,128]{1,0:T(8,128)(4,1)S(1)}, pred[9,128]{1,0:T(8,128)(4,1)}, u32[]{:S(2)}) copy-start(pred[9,128]{1,0:T(8,128)(4,1)} %copy-done.23) | copy-start | bytes 3460
  39.2 6.4 %collective-permute-start.7 = (f32[32,6,8,1]{0,2,3,1:T(8,128)S(1)}, f32[32,6,8,1]{0,2,3,1:T(8,128)S(1)}, u32[]{:S(2)}, u32[]{:S(2)}) collective-permute-start(f32[32,6,8,1]{0,2,3,1:T(8,128)S(1)} %copy.14), channel_id=1, source_target_pairs={{1,0},{2,1},{3,2},{5,4},{6,5},{7,6},{9,8},{10,9},{11,10},{13,12},{... | collective-permute-start | bytes 18440 | tf_op jit(solution)/shard_map/ppermute | solution.py:12
  40.5 6.2 %collective-permute-start.6 = (f32[32,6,1,128]{3,0,2,1:T(8,128)S(1)}, f32[32,6,1,128]{3,0,2,1:T(8,128)S(1)}, u32[]{:S(2)}, u32[]{:S(2)}) collective-permute-start(f32[32,6,1,128]{3,0,2,1:T(8,128)S(1)} %slice.781), channel_id=1, source_target_pairs={{4,0},{8,4},{12,8},{16,12},{20,16},{24,20},{28,24},{32,28},{36,32}... | collective-permute-start | bytes 294920 | tf_op jit(solution)/shard_map/ppermute | solution.py:12
  44.4 3.9 copy-start.17
  48.4 10.6 %copy-start.1 = (f32[32,6,8,128]{3,0,2,1:T(8,128)}, f32[32,6,8,128]{3,0,2,1:T(8,128)S(1)}, u32[]{:S(2)}) copy-start(f32[32,6,8,128]{3,0,2,1:T(8,128)S(1)} %broadcast_multiply_fusion.3) | copy-start | bytes 2359300
  48.4 2.8 copy-start.9
  49.1 12.4 %collective-permute-start.8 = (f32[32,6,1,128]{3,0,2,1:T(8,128)}, f32[32,6,1,128]{3,0,2,1:T(8,128)}, u32[]{:S(2)}, u32[]{:S(2)}) collective-permute-start(f32[32,6,1,128]{3,0,2,1:T(8,128)} %slice.784), channel_id=1, source_target_pairs={{0,4},{4,8},{8,12},{12,16},{16,20},{20,24},{24,28},{28,32},{32,36}... | collective-permute-start | bytes 294920 | tf_op jit(solution)/shard_map/ppermute | solution.py:12
  54.6 4.9 %collective-permute-start.9 = (f32[32,6,8,1]{0,2,3,1:T(8,128)}, f32[32,6,8,1]{0,2,3,1:T(8,128)}, u32[]{:S(2)}, u32[]{:S(2)}) collective-permute-start(f32[32,6,8,1]{0,2,3,1:T(8,128)} %copy.16), channel_id=1, source_target_pairs={{0,1},{1,2},{2,3},{4,5},{5,6},{6,7},{8,9},{9,10},{10,11},{12,13},{... | collective-permute-start | bytes 18440 | tf_op jit(solution)/shard_map/ppermute | solution.py:12
  59.0 2.5 slice-start.1
  278.9 9.0 %collective-permute-start.10 = (f32[32,6,1,128]{3,0,2,1:T(8,128)S(1)}, f32[32,6,1,128]{3,0,2,1:T(8,128)S(1)}, u32[]{:S(2)}, u32[]{:S(2)}) collective-permute-start(f32[32,6,1,128]{3,0,2,1:T(8,128)S(1)} %slice.795), channel_id=1, source_target_pairs={{4,0},{8,4},{12,8},{16,12},{20,16},{24,20},{28,24},{32,28},{36,32}... | collective-permute-start | bytes 294920 | tf_op jit(solution)/shard_map/ppermute | solution.py:12
  281.8 4.8 %collective-permute-start.11 = (f32[32,6,8,1]{0,2,3,1:T(8,128)S(1)}, f32[32,6,8,1]{0,2,3,1:T(8,128)S(1)}, u32[]{:S(2)}, u32[]{:S(2)}) collective-permute-start(f32[32,6,8,1]{0,2,3,1:T(8,128)S(1)} %copy.18), channel_id=1, source_target_pairs={{1,0},{2,1},{3,2},{5,4},{6,5},{7,6},{9,8},{10,9},{11,10},{13,12},{... | collective-permute-start | bytes 18440 | tf_op jit(solution)/shard_map/ppermute | solution.py:12
  291.4 13.3 %collective-permute-start.12 = (f32[32,6,1,128]{3,0,2,1:T(8,128)}, f32[32,6,1,128]{3,0,2,1:T(8,128)}, u32[]{:S(2)}, u32[]{:S(2)}) collective-permute-start(f32[32,6,1,128]{3,0,2,1:T(8,128)} %slice.798), channel_id=1, source_target_pairs={{0,4},{4,8},{8,12},{12,16},{16,20},{20,24},{24,28},{28,32},{32,36}... | collective-permute-start | bytes 294920 | tf_op jit(solution)/shard_map/ppermute | solution.py:12
  298.6 4.9 %collective-permute-start.13 = (f32[32,6,8,1]{0,2,3,1:T(8,128)S(1)}, f32[32,6,8,1]{0,2,3,1:T(8,128)S(1)}, u32[]{:S(2)}, u32[]{:S(2)}) collective-permute-start(f32[32,6,8,1]{0,2,3,1:T(8,128)S(1)} %copy.20), channel_id=1, source_target_pairs={{0,1},{1,2},{2,3},{4,5},{5,6},{6,7},{8,9},{9,10},{10,11},{12,13},{... | collective-permute-start | bytes 18440 | tf_op jit(solution)/shard_map/ppermute | solution.py:12
  (22 other events, 19.8 us)
where the time goes:
time: 415 us; the launch traced here: 413 us
  blocking collectives  312 us (75%)
  starting transfers between devices  41.7 us (10%)
  local copies, waits for them, and re-layouts  31.7 us (8%)
  other arithmetic  21.5 us (5%)
  waiting for transfers between devices  4.56 us (1%)
    psum x2, blocking collectives, inner_rz(): return lax.psum(jnp.sum(first * second, axis=(1, 2, 3)), ('slab', 'sub'))  212 us
    psum x1, blocking collectives, inner_pq(): return lax.psum(jnp.sum(first * second, axis=(1, 2, 3)), ('slab', 'sub'))  101 us
    ppermute x14, starting transfers between devices, from_behind(): lax.ppermute(value, axis, [(source, source + steps) for source in range(i...  41.7 us
    unnamed x64, local copies, waits for them, and re-layouts  10.6 us
  transfers between devices with their start and end apart: 14, of which 4 were waited for; matrix products, arithmetic and copies ran while one was open for 6% of the time, Pallas kernels for 0%

commit v1 on v0

--- a/solution.py
+++ b/solution.py
@@ -79,7 +79,7 @@
 
 
 def inner_rz(first, second):
-    return lax.psum(jnp.sum(first * second, axis=(1, 2, 3)), ("slab", "sub"))
+    return jnp.sum(lax.all_gather(jnp.sum(first * second, axis=(1, 2, 3)), ("slab", "sub")), axis=0)
 
 
 def inner_pq(first, second):

time: 415 us -> 1100 us (2.65)
  waiting for transfers between devices: 4.56 us -> 773 us
  blocking collectives: 312 us -> 215 us
  between operations: 1.34 us -> 14.8 us
    unnamed x0 -> x4, waiting for transfers between devices: none -> 769 us
    psum x2 -> x0, blocking collectives: 212 us -> none  [inner_rz(): return lax.psum(jnp.sum(first * second, axis=(1, 2, 3)), ('slab', 'sub'))]
    psum x1 -> x2, blocking collectives: 101 us -> 215 us  [inner_pq(): return lax.psum(jnp.sum(first * second, axis=(1, 2, 3)), ('slab', 'sub'))]
  transfers between devices with their start and end apart: 14 -> 16, of which waited for: 4 -> 6; matrix products, arithmetic and copies ran while one was open for 6% -> 2% of each run, Pallas kernels for 0% -> 0%
where the time goes in v1:
time: 1100 us
  waiting for transfers between devices  773 us (70%)
  blocking collectives  215 us (20%)
  starting transfers between devices  40.9 us (4%)
  local copies, waits for them, and re-layouts  34.7 us (3%)
  other arithmetic  21.7 us (2%)
  between operations  14.8 us (1%)
    unnamed x4, waiting for transfers between devices  769 us
    psum x2, blocking collectives, inner_pq(): return lax.psum(jnp.sum(first * second, axis=(1, 2, 3)), ('slab', 'sub'))  215 us
    ppermute x14, starting transfers between devices, from_behind(): lax.ppermute(value, axis, [(source, source + steps) for source in range(i...  40.8 us
  transfers between devices with their start and end apart: 16, of which 6 were waited for; matrix products, arithmetic and copies ran while one was open for 2% of the time, Pallas kernels for 0%

profile of v1, /device:TPU:1, one launch (start us, length us, event | category | flops | bytes accessed | tf_op | source)
XLA Modules:
  0.0 1099.9 jit_solution(17322523447961775440)
XLA Ops:
  8.0 4.9 collective-permute-start.4
  13.7 3.1 collective-permute-start.5
  19.6 3.3 collective-permute-start
  34.4 2.2 collective-permute-start.1
  37.4 4.0 collective-permute-start.3
  47.1 3.8 collective-permute-start.6
  53.3 1.6 fusion.9
  55.7 2.1 collective-permute-start.8
  59.1 2.1 copy.16
  61.2 4.4 collective-permute-start.9
  66.1 2.0 copy.17
  68.1 2.6 multiply_reduce_fusion.2
  71.7 113.3 %psum.14 = f32[32]{0:T(128)S(1)} all-reduce(f32[32]{0:T(128)S(1)} %get-tuple-element.6), channel_id=1, replica_groups=mesh['slab'=128,'sub'=4] {'slab','sub'}, use_global_device_ids=true, to_apply=%region_7.0 | all-reduce | flops 32 | bytes 256 | tf_op jit(solution)/shard_map/psum | solution.py:86
  185.0 335.1 %all-reduce.5.cloned.1.call-done = f32[16384]{0:T(1024)} async-done(((f32[16384]{0:T(1024)}), f32[16384]{0:T(1024)}) %all-reduce.5.cloned.1.call-update) | async-done | bytes 65552
  524.9 433.5 %all-reduce.7.cloned.1.call-done = f32[16384]{0:T(1024)} async-done(((f32[16384]{0:T(1024)}), f32[16384]{0:T(1024)}) %all-reduce.7.cloned.1.call-update) | async-done | bytes 65552
  959.8 2.3 collective-permute-start.10
  964.9 2.3 collective-permute-done.11
  968.5 1.8 fusion.14
  971.4 4.1 collective-permute-start.12
  978.3 2.6 collective-permute-start.13
  980.8 2.0 slice.799
  984.1 2.7 multiply_reduce_fusion
  986.8 101.4 %psum.15 = f32[32]{0:T(128)S(1)} all-reduce(f32[32]{0:T(128)S(1)} %get-tuple-element.12), channel_id=1, replica_groups=mesh['slab'=128,'sub'=4] {'slab','sub'}, use_global_device_ids=true, to_apply=%region_13.0 | all-reduce | flops 32 | bytes 256 | tf_op jit(solution)/shard_map/psum | solution.py:86
  1088.9 1.5 multiply_subtract_fusion
  (184 shorter events, 46.3 us)
Async XLA Ops:
  7.2 512.9 %all-reduce.5.cloned.1.call-start = ((), (), s32[]{:S(2)}) async-start(), calls=%async_computation | async-start | bytes 131072
  8.0 20.2 %collective-permute-start.4 = (f32[6,1,128]{2,1,0:T(1,128)S(1)}, f32[6,1,128]{2,1,0:T(1,128)S(1)}, u32[]{:S(2)}, u32[]{:S(2)}) collective-permute-start(f32[6,1,128]{2,1,0:T(1,128)S(1)} %slice.527), channel_id=1, source_target_pairs={{0,4},{4,8},{8,12},{12,16},{16,20},{20,24},{24,28},{28,32},{32,36}... | collective-permute-start | bytes 9224 | tf_op jit(solution)/shard_map/ppermute | solution.py:12
  13.7 13.8 %collective-permute-start.5 = (f32[6,8,1]{2,1,0:T(8,128)S(1)}, f32[6,8,1]{2,1,0:T(8,128)S(1)}, u32[]{:S(2)}, u32[]{:S(2)}) collective-permute-start(f32[6,8,1]{2,1,0:T(8,128)S(1)} %slice.531), channel_id=1, source_target_pairs={{0,1},{1,2},{2,3},{4,5},{5,6},{6,7},{8,9},{9,10},{10,11},{12,13},{... | collective-permute-start | bytes 584 | tf_op jit(solution)/shard_map/ppermute | solution.py:12
  18.3 14.3 %collective-permute-start.2 = (f32[32,6,8,1]{0,2,3,1:T(8,128)S(1)}, f32[32,6,8,1]{0,2,3,1:T(8,128)S(1)}, u32[]{:S(2)}, u32[]{:S(2)}) collective-permute-start(f32[32,6,8,1]{0,2,3,1:T(8,128)S(1)} %copy.10), channel_id=1, source_target_pairs={{1,0},{2,1},{3,2},{5,4},{6,5},{7,6},{9,8},{10,9},{11,10},{13,12},{... | collective-permute-start | bytes 18440 | tf_op jit(solution)/shard_map/ppermute | solution.py:12
  19.6 13.4 %collective-permute-start = (f32[32,6,1,128]{3,0,2,1:T(8,128)S(1)}, f32[32,6,1,128]{3,0,2,1:T(8,128)S(1)}, u32[]{:S(2)}, u32[]{:S(2)}) collective-permute-start(f32[32,6,1,128]{3,0,2,1:T(8,128)S(1)} %slice.661), channel_id=1, source_target_pairs={{4,0},{8,4},{12,8},{16,12},{20,16},{24,20},{28,24},{32,28},{36,32}... | collective-permute-start | bytes 294920 | tf_op jit(solution)/shard_map/ppermute | solution.py:12
  28.2 3.1 copy-start.9
  34.4 7.1 copy-start.1
  34.4 8.3 collective-permute-start.1
  37.1 4.4 copy-start.10
  37.1 4.4 copy-start.22
  37.4 4.9 collective-permute-start.3
  45.4 5.5 copy-start.26
  45.8 6.4 collective-permute-start.7
  47.1 6.2 collective-permute-start.6
  50.9 3.9 copy-start.19
  55.0 10.6 copy-start
  55.0 2.8 copy-start.11
  55.7 12.4 %collective-permute-start.8 = (f32[32,6,1,128]{3,0,2,1:T(8,128)}, f32[32,6,1,128]{3,0,2,1:T(8,128)}, u32[]{:S(2)}, u32[]{:S(2)}) collective-permute-start(f32[32,6,1,128]{3,0,2,1:T(8,128)} %slice.784), channel_id=1, source_target_pairs={{0,4},{4,8},{8,12},{12,16},{16,20},{20,24},{24,28},{28,32},{32,36}... | collective-permute-start | bytes 294920 | tf_op jit(solution)/shard_map/ppermute | solution.py:12
  61.2 4.9 collective-permute-start.9
  71.6 886.8 %all-reduce.7.cloned.1.call-start = ((), (), s32[]{:S(2)}) async-start(), calls=%async_computation.1 | async-start | bytes 131072
  959.8 8.7 collective-permute-start.10
  962.5 4.8 collective-permute-start.11
  971.4 12.7 %collective-permute-start.12 = (f32[32,6,1,128]{3,0,2,1:T(8,128)}, f32[32,6,1,128]{3,0,2,1:T(8,128)}, u32[]{:S(2)}, u32[]{:S(2)}) collective-permute-start(f32[32,6,1,128]{3,0,2,1:T(8,128)} %slice.798), channel_id=1, source_target_pairs={{0,4},{4,8},{8,12},{12,16},{16,20},{20,24},{24,28},{28,32},{32,36}... | collective-permute-start | bytes 294920 | tf_op jit(solution)/shard_map/ppermute | solution.py:12
  978.3 4.6 collective-permute-start.13
  (26 other events, 26.9 us)
Sparse Core Ops, SparseCore 0:
  71.8 448.2 all-reduce.4
  527.0 431.4 all-reduce.6
